TPU v7x, 128 devices: a whole 4x4x4 slice. The times are simulated.
128 devices in a mesh: ctx: 32 (over z, x, y_lo), tp: 4 (over y_hi, core).
Axes of the slice: x: 4, y: 4 (y_hi: 2, y_lo: 2; y = y_hi * 2 + y_lo), z: 4, core: 2. Of those that a mesh axis runs over, the one named last changes fastest.
Arguments:
- signal: bfloat16 [4096, 2048], P('ctx', 'tp'), may hold values from -6 to 6
- gate: bfloat16 [4096, 2048], P('ctx', 'tp'), may hold values from -6 to 6
- filt: bfloat16 [4096, 2048], P('ctx', 'tp'), may hold values from -0.25 to 0.25
- bias: float32 [2048], P('tp'), may hold values from -2 to 2
- doc_ids: int32 [4096], replicated, may hold values from 0 to 3, never falling along the last dimension, each value on 1 to 3840 neighbouring positions
- block_perm: int32 [64], replicated, may hold values from 0 to 63, each once
- out_weight: bfloat16 [2048, 2048], P('tp'), may hold values from -0.125 to 0.125
Outputs:
- mixed: bfloat16 [4096, 2048], P('ctx', 'tp')
Inputs may be any that keep to these rules, and one draw needn't show every extreme that they name: `doc_ids`: ids never fall along the sequence; each document is a run of 1 to 3840 positions, one exactly 3840. `block_perm`: each block number once.
All inputs are finite; a program needn't handle non-finite values.
Results may differ from a plain program's by a relative error of at most 0.012.
Values may be sent and summed in bfloat16 or wider, within the bound.
No kernel may reach another device: no remote copies, remote signals or barrier semaphores. Data moves between devices by JAX's collectives and lax.ppermute only.
A program may use at most 64 MiB of HBM per device.

v0:
```python
import jax
import jax.numpy as jnp
from jax import lax
from jax.sharding import PartitionSpec as P

SPAN = 64
DOC_COUNT = 4


def skew_blocks(a, fill):
    chans, blocks, span = a.shape
    a_ext = jnp.concatenate([a, jnp.full_like(a, fill)], axis=1)
    tiled = jnp.broadcast_to(a_ext[:, None], (chans, blocks, 2 * blocks, span))
    tiled = tiled.reshape(chans, blocks * 2 * blocks, span)[:, : blocks * (2 * blocks - 1)]
    return tiled.reshape(chans, blocks, 2 * blocks - 1, span)[:, :, :blocks]


def block_conv(x_cm, f_cm, doc_ids):
    chans, seq = x_cm.shape
    span = SPAN
    blocks = seq // span
    width = seq + span
    f_ext = jnp.pad(f_cm, ((0, 0), (0, span)))
    tt = jnp.broadcast_to(f_ext[:, None, :], (chans, span, width)).reshape(chans, span * width)
    tt = tt[:, : span * (width - 1)].reshape(chans, span, width - 1)[:, :, :seq]
    tt = tt.reshape(chans, span, blocks, span)
    xb = x_cm.reshape(chans, blocks, span)
    src = skew_blocks(xb, 0)
    docb = doc_ids.reshape(blocks, span)
    lead = docb[:, 0]
    src_doc = skew_blocks(docb[None], -1)[0]
    keep = src_doc == lead[None, :, None]
    src = jnp.where(keep[None], src, jnp.zeros_like(src))
    lead_part = jnp.einsum("cjdi,cdtj->cit", tt, src, preferred_element_type=jnp.float32)
    row_doc = docb.T
    lead_rows = row_doc == lead[None, :]
    out = jnp.where(lead_rows[None], lead_part, 0.0)
    near = tt[:, :, 0, :]
    xt = jnp.swapaxes(xb, 1, 2)
    for doc in range(DOC_COUNT):
        member = docb.T == doc
        part = jnp.einsum(
            "cji,cjt->cit",
            near,
            jnp.where(member[None], xt, jnp.zeros_like(xt)),
            preferred_element_type=jnp.float32,
        )
        rows = member & (lead[None, :] != doc)
        out = out + jnp.where(rows[None], part, 0.0)
    return jnp.swapaxes(out, 1, 2).reshape(chans, seq)


def body(signal, gate, filt, bias, doc_ids, block_perm, out_weight):
    span = SPAN
    rows, chans = signal.shape
    blocks = block_perm.shape[0]
    seq = blocks * span
    n_ctx = seq // rows
    per_dev = chans // n_ctx
    ctx_index = lax.axis_index("ctx")

    def to_channel_major(a):
        return lax.all_to_all(a, "ctx", 1, 0, tiled=True).T

    inverse = (
        jnp.zeros((blocks,), jnp.int32).at[block_perm].set(jnp.arange(blocks, dtype=jnp.int32))
    )

    def slots_to_natural(a):
        return jnp.take(a.reshape(per_dev, blocks, span), inverse, axis=1).reshape(per_dev, seq)

    x_cm = slots_to_natural(to_channel_major(signal))
    g_cm = slots_to_natural(to_channel_major(gate))
    f_cm = to_channel_major(filt)
    bias_cm = lax.dynamic_slice_in_dim(bias, ctx_index * per_dev, per_dev)
    group = 4
    conv = lax.map(
        lambda xf: block_conv(xf[0], xf[1], doc_ids),
        (x_cm.reshape(per_dev // group, group, seq), f_cm.reshape(per_dev // group, group, seq)),
    ).reshape(per_dev, seq)
    gated = (
        g_cm.astype(jnp.float32) * (conv + bias_cm[:, None] * x_cm.astype(jnp.float32))
    ).astype(jnp.bfloat16)
    gated_slots = jnp.take(gated.reshape(per_dev, blocks, span), block_perm, axis=1)
    gated_slots = gated_slots.reshape(per_dev, seq).T
    gated_local = lax.all_to_all(gated_slots, "ctx", 0, 1, tiled=True)
    partial_value = jnp.dot(gated_local, out_weight, preferred_element_type=jnp.float32)
    return lax.psum_scatter(partial_value, "tp", scatter_dimension=1, tiled=True).astype(
        jnp.bfloat16
    )


def solution(mesh):
    return jax.shard_map(
        body,
        mesh=mesh,
        in_specs=(P("ctx", "tp"), P("ctx", "tp"), P("ctx", "tp"), P("tp"), P(), P(), P("tp", None)),
        out_specs=P("ctx", "tp"),
        check_vma=False,
    )
```

profile of v0, /device:TPU:1, one launch (start us, length us, event | category | flops | bytes accessed | tf_op | source)
XLA Modules:
  0.0 430.1 jit_solution(5247840323906330248)
XLA Ops:
  8.3 9.7 %all-to-all-start.1 = ((bf16[128,32,16]{0,2,1:T(8,128)(2,1)}), bf16[128,32,16]{0,2,1:T(8,128)(2,1)S(1)}, u32[]{:S(2)}, u32[]{:S(2)}) async-start(bf16[128,32,16]{0,2,1:T(8,128)(2,1)} %bitcast.15), calls=%async_computation.1 | async-start | bytes 262144 | tf_op jit(solution)/shard_map/all_to_all | solution.py:63
  25.7 6.9 %all-to-all-start.2 = ((bf16[128,32,16]{0,2,1:T(8,128)(2,1)}), bf16[128,32,16]{0,2,1:T(8,128)(2,1)S(1)}, u32[]{:S(2)}, u32[]{:S(2)}) async-start(bf16[128,32,16]{0,2,1:T(8,128)(2,1)} %bitcast.19), calls=%async_computation.2 | async-start | bytes 262144 | tf_op jit(solution)/shard_map/all_to_all | solution.py:63
  34.2 6.1 %all-to-all-done.2 = bf16[128,32,16]{0,2,1:T(8,128)(2,1)S(1)} async-done(((bf16[128,32,16]{0,2,1:T(8,128)(2,1)}), bf16[128,32,16]{0,2,1:T(8,128)(2,1)S(1)}, u32[]{:S(2)}, u32[]{:S(2)}) %all-to-all-start.2) | async-done | bytes 131104 | tf_op jit(solution)/shard_map/all_to_all | solution.py:63
  40.2 3.9 all-to-all-start
  44.2 323.2 %while.12 = (s32[]{:T(128)}, f32[4,4,4096]{2,1,0:T(4,128)}, s32[4096]{0:T(1024)S(1)}, bf16[4,4,4096]{2,1,0:T(4,128)(2,1)S(1)}, bf16[4,4,4096]{2,1,0:T(4,128)(2,1)S(1)}, /*index=5*/s32[]{:T(128)}, bf16[]{:T(256)}) while((s32[]{:T(128)}, f32[4,4,4096]{2,1,0:T(4,128)}, s32[4096]{0:T(1024)S(1)}, bf16[4,4,4096]{2,1,0:T(4,128)(2,1)S(1)}, ...), condition=%wide.region_2.4_spmd, body=%wide.region_1.0_spmd.sunk | while | flops 144167168 | bytes 68822360 | solution.py:77
  46.3 4.7 %reshape.231 = bf16[1064960]{0:T(1024)(128)(2,1)} reshape(bf16[4,64,4160]{2,1,0:T(8,128)(2,1)} %broadcast_in_dim.225) | data formatting | bytes 4259840 | tf_op jit(solution)/shard_map/while
  50.9 3.7 reshape.232
  54.7 4.5 %reshape.233 = bf16[1064704]{0:T(1024)(128)(2,1)} reshape(bf16[4,266176]{1,0:T(4,128)(2,1)} %bitcast.134) | data formatting | bytes 4258816 | tf_op jit(solution)/shard_map/while
  59.2 6.4 %reshape.234 = bf16[4,64,4159]{2,1,0:T(8,128)(2,1)} reshape(bf16[1064704]{0:T(1024)(128)(2,1)} %reshape.233) | data formatting | bytes 4258816 | tf_op jit(solution)/shard_map/while/body/eval_jaxpr/reshape | solution.py:25
  65.6 3.1 slice.80
  68.8 6.9 %reshape.235 = bf16[4,64,64,64]{3,2,1,0:T(8,128)(2,1)} reshape(bf16[4,64,4096]{2,1,0:T(8,128)(2,1)} %slice.80) | data formatting | bytes 4194304 | tf_op jit(solution)/shard_map/while/body/eval_jaxpr/reshape | solution.py:26
  80.0 7.3 %reshape.238 = bf16[4,8192,64]{1,2,0:T(8,128)(2,1)} reshape(bf16[4,64,128,64]{2,1,3,0:T(8,128)(2,1)} %broadcast_in_dim.226) | data formatting | bytes 8388608 | tf_op jit(solution)/shard_map/while/body/eval_jaxpr/reshape | solution.py:14
  87.4 19.3 %reshape.239 = bf16[4,64,127,64]{2,1,3,0:T(8,128)(2,1)} reshape(bf16[4,8128,64]{1,2,0:T(8,128)(2,1)} %bitcast.133) | data formatting | bytes 8323072 | tf_op jit(solution)/shard_map/while/body/eval_jaxpr/reshape | solution.py:15
  108.3 2.8 broadcast_in_dim.228
  111.1 6.4 %reshape.241 = s32[1,64,127,64]{2,1,3,0:T(8,128)} reshape(s32[1,8128,64]{1,2,0:T(8,128)} %bitcast.135) | data formatting | bytes 4161536 | tf_op jit(solution)/shard_map/while/body/eval_jaxpr/reshape | solution.py:15
  119.4 4.9 %fusion.53 = f32[4,64,64]{2,1,0:T(8,128)S(1)} fusion(bf16[4,64,64,64]{3,2,1,0:T(8,128)(2,1)} %reshape.235, bf16[4,64,127,64]{2,1,3,0:T(8,128)(2,1)} %reshape.239, pred[64,64,64]{1,0,2:T(8,128)(4,1)S(1)} %fusion.52, pred[64,64]{1,0:T(8,128)(4,1)S(1)} %get-tuple-element.155), kind=kOutput, calls=%fused_computation.19.clone.1 | convolution fusion | flops 135282688 | bytes 6590464 | tf_op jit(solution)/shard_map/while/body/eval_jaxpr/cjdi,cdtj->cit/dot_general | solution.py:34
  127.0 4.7 %reshape.231 = bf16[1064960]{0:T(1024)(128)(2,1)} reshape(bf16[4,64,4160]{2,1,0:T(8,128)(2,1)} %broadcast_in_dim.225) | data formatting | bytes 4259840 | tf_op jit(solution)/shard_map/while
  131.7 3.7 reshape.232
  135.4 4.5 %reshape.233 = bf16[1064704]{0:T(1024)(128)(2,1)} reshape(bf16[4,266176]{1,0:T(4,128)(2,1)} %bitcast.134) | data formatting | bytes 4258816 | tf_op jit(solution)/shard_map/while
  140.0 6.4 %reshape.234 = bf16[4,64,4159]{2,1,0:T(8,128)(2,1)} reshape(bf16[1064704]{0:T(1024)(128)(2,1)} %reshape.233) | data formatting | bytes 4258816 | tf_op jit(solution)/shard_map/while/body/eval_jaxpr/reshape | solution.py:25
  146.4 3.1 slice.80
  149.5 6.9 %reshape.235 = bf16[4,64,64,64]{3,2,1,0:T(8,128)(2,1)} reshape(bf16[4,64,4096]{2,1,0:T(8,128)(2,1)} %slice.80) | data formatting | bytes 4194304 | tf_op jit(solution)/shard_map/while/body/eval_jaxpr/reshape | solution.py:26
  160.8 7.3 %reshape.238 = bf16[4,8192,64]{1,2,0:T(8,128)(2,1)} reshape(bf16[4,64,128,64]{2,1,3,0:T(8,128)(2,1)} %broadcast_in_dim.226) | data formatting | bytes 8388608 | tf_op jit(solution)/shard_map/while/body/eval_jaxpr/reshape | solution.py:14
  168.1 19.3 %reshape.239 = bf16[4,64,127,64]{2,1,3,0:T(8,128)(2,1)} reshape(bf16[4,8128,64]{1,2,0:T(8,128)(2,1)} %bitcast.133) | data formatting | bytes 8323072 | tf_op jit(solution)/shard_map/while/body/eval_jaxpr/reshape | solution.py:15
  191.8 6.4 %reshape.241 = s32[1,64,127,64]{2,1,3,0:T(8,128)} reshape(s32[1,8128,64]{1,2,0:T(8,128)} %bitcast.135) | data formatting | bytes 4161536 | tf_op jit(solution)/shard_map/while/body/eval_jaxpr/reshape | solution.py:15
  200.1 4.9 %fusion.53 = f32[4,64,64]{2,1,0:T(8,128)S(1)} fusion(bf16[4,64,64,64]{3,2,1,0:T(8,128)(2,1)} %reshape.235, bf16[4,64,127,64]{2,1,3,0:T(8,128)(2,1)} %reshape.239, pred[64,64,64]{1,0,2:T(8,128)(4,1)S(1)} %fusion.52, pred[64,64]{1,0:T(8,128)(4,1)S(1)} %get-tuple-element.155), kind=kOutput, calls=%fused_computation.19.clone.1 | convolution fusion | flops 135282688 | bytes 6590464 | tf_op jit(solution)/shard_map/while/body/eval_jaxpr/cjdi,cdtj->cit/dot_general | solution.py:34
  207.8 4.7 %reshape.231 = bf16[1064960]{0:T(1024)(128)(2,1)} reshape(bf16[4,64,4160]{2,1,0:T(8,128)(2,1)} %broadcast_in_dim.225) | data formatting | bytes 4259840 | tf_op jit(solution)/shard_map/while
  212.5 3.7 reshape.232
  216.2 4.5 %reshape.233 = bf16[1064704]{0:T(1024)(128)(2,1)} reshape(bf16[4,266176]{1,0:T(4,128)(2,1)} %bitcast.134) | data formatting | bytes 4258816 | tf_op jit(solution)/shard_map/while
  220.7 6.4 %reshape.234 = bf16[4,64,4159]{2,1,0:T(8,128)(2,1)} reshape(bf16[1064704]{0:T(1024)(128)(2,1)} %reshape.233) | data formatting | bytes 4258816 | tf_op jit(solution)/shard_map/while/body/eval_jaxpr/reshape | solution.py:25
  227.2 3.1 slice.80
  230.3 6.9 %reshape.235 = bf16[4,64,64,64]{3,2,1,0:T(8,128)(2,1)} reshape(bf16[4,64,4096]{2,1,0:T(8,128)(2,1)} %slice.80) | data formatting | bytes 4194304 | tf_op jit(solution)/shard_map/while/body/eval_jaxpr/reshape | solution.py:26
  241.6 7.3 %reshape.238 = bf16[4,8192,64]{1,2,0:T(8,128)(2,1)} reshape(bf16[4,64,128,64]{2,1,3,0:T(8,128)(2,1)} %broadcast_in_dim.226) | data formatting | bytes 8388608 | tf_op jit(solution)/shard_map/while/body/eval_jaxpr/reshape | solution.py:14
  248.9 19.3 %reshape.239 = bf16[4,64,127,64]{2,1,3,0:T(8,128)(2,1)} reshape(bf16[4,8128,64]{1,2,0:T(8,128)(2,1)} %bitcast.133) | data formatting | bytes 8323072 | tf_op jit(solution)/shard_map/while/body/eval_jaxpr/reshape | solution.py:15
  272.6 6.4 %reshape.241 = s32[1,64,127,64]{2,1,3,0:T(8,128)} reshape(s32[1,8128,64]{1,2,0:T(8,128)} %bitcast.135) | data formatting | bytes 4161536 | tf_op jit(solution)/shard_map/while/body/eval_jaxpr/reshape | solution.py:15
  280.9 4.9 %fusion.53 = f32[4,64,64]{2,1,0:T(8,128)S(1)} fusion(bf16[4,64,64,64]{3,2,1,0:T(8,128)(2,1)} %reshape.235, bf16[4,64,127,64]{2,1,3,0:T(8,128)(2,1)} %reshape.239, pred[64,64,64]{1,0,2:T(8,128)(4,1)S(1)} %fusion.52, pred[64,64]{1,0:T(8,128)(4,1)S(1)} %get-tuple-element.155), kind=kOutput, calls=%fused_computation.19.clone.1 | convolution fusion | flops 135282688 | bytes 6590464 | tf_op jit(solution)/shard_map/while/body/eval_jaxpr/cjdi,cdtj->cit/dot_general | solution.py:34
  288.6 4.7 %reshape.231 = bf16[1064960]{0:T(1024)(128)(2,1)} reshape(bf16[4,64,4160]{2,1,0:T(8,128)(2,1)} %broadcast_in_dim.225) | data formatting | bytes 4259840 | tf_op jit(solution)/shard_map/while
  293.2 3.7 reshape.232
  297.0 4.5 %reshape.233 = bf16[1064704]{0:T(1024)(128)(2,1)} reshape(bf16[4,266176]{1,0:T(4,128)(2,1)} %bitcast.134) | data formatting | bytes 4258816 | tf_op jit(solution)/shard_map/while
  301.5 6.4 %reshape.234 = bf16[4,64,4159]{2,1,0:T(8,128)(2,1)} reshape(bf16[1064704]{0:T(1024)(128)(2,1)} %reshape.233) | data formatting | bytes 4258816 | tf_op jit(solution)/shard_map/while/body/eval_jaxpr/reshape | solution.py:25
  307.9 3.1 slice.80
  311.0 6.9 %reshape.235 = bf16[4,64,64,64]{3,2,1,0:T(8,128)(2,1)} reshape(bf16[4,64,4096]{2,1,0:T(8,128)(2,1)} %slice.80) | data formatting | bytes 4194304 | tf_op jit(solution)/shard_map/while/body/eval_jaxpr/reshape | solution.py:26
  322.3 7.3 %reshape.238 = bf16[4,8192,64]{1,2,0:T(8,128)(2,1)} reshape(bf16[4,64,128,64]{2,1,3,0:T(8,128)(2,1)} %broadcast_in_dim.226) | data formatting | bytes 8388608 | tf_op jit(solution)/shard_map/while/body/eval_jaxpr/reshape | solution.py:14
  329.7 19.3 %reshape.239 = bf16[4,64,127,64]{2,1,3,0:T(8,128)(2,1)} reshape(bf16[4,8128,64]{1,2,0:T(8,128)(2,1)} %bitcast.133) | data formatting | bytes 8323072 | tf_op jit(solution)/shard_map/while/body/eval_jaxpr/reshape | solution.py:15
  353.4 6.4 %reshape.241 = s32[1,64,127,64]{2,1,3,0:T(8,128)} reshape(s32[1,8128,64]{1,2,0:T(8,128)} %bitcast.135) | data formatting | bytes 4161536 | tf_op jit(solution)/shard_map/while/body/eval_jaxpr/reshape | solution.py:15
  361.6 4.9 %fusion.53 = f32[4,64,64]{2,1,0:T(8,128)S(1)} fusion(bf16[4,64,64,64]{3,2,1,0:T(8,128)(2,1)} %reshape.235, bf16[4,64,127,64]{2,1,3,0:T(8,128)(2,1)} %reshape.239, pred[64,64,64]{1,0,2:T(8,128)(4,1)S(1)} %fusion.52, pred[64,64]{1,0:T(8,128)(4,1)S(1)} %get-tuple-element.155), kind=kOutput, calls=%fused_computation.19.clone.1 | convolution fusion | flops 135282688 | bytes 6590464 | tf_op jit(solution)/shard_map/while/body/eval_jaxpr/cjdi,cdtj->cit/dot_general | solution.py:34
  372.1 15.1 %all_to_all.76 = bf16[32,128,16]{1,2,0:T(8,128)(2,1)S(1)} all-to-all(bf16[32,128,16]{1,2,0:T(8,128)(2,1)S(1)} %copy_bitcast_fusion.1), channel_id=1, replica_groups=mesh['ctx'=32,'tp'=4] {'ctx'}, dimensions={0} | all-to-all | bytes 262144 | tf_op jit(solution)/shard_map/all_to_all | solution.py:86
  388.6 33.0 %reduce-scatter.2.cloned.1.call-done = f32[128,512]{1,0:T(8,128)} async-done(((f32[128,2048]{1,0:T(8,128)}), f32[128,512]{1,0:T(8,128)}) %reduce-scatter.2.cloned.1.call-update) | async-done | bytes 262160 | tf_op jit(solution)/shard_map/reduce_scatter | solution.py:88
  (146 shorter events, 69.4 us)
Async XLA Ops:
  6.5 380.6 %copy-start = (bf16[512,2048]{1,0:T(8,128)(2,1)S(1)}, bf16[512,2048]{1,0:T(8,128)(2,1)}, u32[]{:S(2)}) copy-start(bf16[512,2048]{1,0:T(8,128)(2,1)} %param.17) | copy-start | bytes 6291460
  8.3 17.3 %all-to-all-start.1 = ((bf16[128,32,16]{0,2,1:T(8,128)(2,1)}), bf16[128,32,16]{0,2,1:T(8,128)(2,1)S(1)}, u32[]{:S(2)}, u32[]{:S(2)}) async-start(bf16[128,32,16]{0,2,1:T(8,128)(2,1)} %bitcast.15), calls=%async_computation.1 | async-start | bytes 262144 | tf_op jit(solution)/shard_map/all_to_all | solution.py:63
  23.6 20.7 %copy-start.1 = (s32[4096]{0:T(1024)S(1)}, s32[4096]{0:T(1024)}, u32[]{:S(2)}) copy-start(s32[4096]{0:T(1024)} %param.15) | copy-start | bytes 49156
  25.7 14.5 %all-to-all-start.2 = ((bf16[128,32,16]{0,2,1:T(8,128)(2,1)}), bf16[128,32,16]{0,2,1:T(8,128)(2,1)S(1)}, u32[]{:S(2)}, u32[]{:S(2)}) async-start(bf16[128,32,16]{0,2,1:T(8,128)(2,1)} %bitcast.19), calls=%async_computation.2 | async-start | bytes 262144 | tf_op jit(solution)/shard_map/all_to_all | solution.py:63
  40.2 328.5 %all-to-all-start = ((bf16[128,32,16]{0,2,1:T(8,128)(2,1)}), bf16[128,32,16]{0,2,1:T(8,128)(2,1)S(1)}, u32[]{:S(2)}, u32[]{:S(2)}) async-start(bf16[128,32,16]{0,2,1:T(8,128)(2,1)} %bitcast.11), calls=%async_computation | async-start | bytes 262144 | tf_op jit(solution)/shard_map/all_to_all | solution.py:63
  44.1 377.6 %reduce-scatter.2.cloned.1.call-start = ((), (), s32[]{:S(2)}) async-start(), calls=%async_computation.5 | async-start | bytes 1310720 | tf_op jit(solution)/shard_map/reduce_scatter | solution.py:88
Sparse Core Ops, SparseCore 0:
  388.7 32.8 reduce-scatter.1
where the time goes:
time: 433 us; the launch traced here: 430 us
  local copies, waits for them, and re-layouts  305 us (70%)
  waiting for transfers between devices  39.9 us (9%)
  matrix products  23.5 us (5%)
  starting transfers between devices  20.6 us (5%)
  blocking collectives  15.1 us (3%)
  between operations  13.6 us (3%)
  other arithmetic  12.4 us (3%)
    reshape x8, local copies, waits for them, and re-layouts, skew_blocks(): return tiled.reshape(chans, blocks, 2 * blocks - 1, span)[:, :, :blocks]  103 us
    while x16, local copies, waits for them, and re-layouts  37.3 us
    reduce_scatter x1, waiting for transfers between devices, body(): lax.psum_scatter(partial_value, 'tp', scatter_dimension=1, tiled=True)  33 us
    reshape x4, local copies, waits for them, and re-layouts, skew_blocks(): tiled.reshape(chans, blocks * 2 * blocks, span)  29.3 us
    reshape x4, local copies, waits for them, and re-layouts, block_conv(): tt = tt.reshape(chans, span, blocks, span)  27.6 us
    broadcast_in_dim x20, local copies, waits for them, and re-layouts, skew_blocks(): tiled = jnp.broadcast_to(a_ext[:, None], (chans, blocks, 2 * blocks, span))  27.4 us
    reshape x4, local copies, waits for them, and re-layouts, block_conv(): tt = tt[:, :span * (width - 1)].reshape(chans, span, width - 1)[:, :, :seq]  25.7 us
    all_to_all x3, starting transfers between devices, to_channel_major(): return lax.all_to_all(a, 'ctx', 1, 0, tiled=True).T  20.5 us
  transfers between devices with their start and end apart: 4, of which 3 were waited for; matrix products, arithmetic and copies ran while one was open for 77% of the time, Pallas kernels for 0%

commit v1 on v0

--- a/solution.py
+++ b/solution.py
@@ -83,7 +83,12 @@
     ).astype(jnp.bfloat16)
     gated_slots = jnp.take(gated.reshape(per_dev, blocks, span), block_perm, axis=1)
     gated_slots = gated_slots.reshape(per_dev, seq).T
-    gated_local = lax.all_to_all(gated_slots, "ctx", 0, 1, tiled=True)
+    gated_local = jnp.concatenate(
+        lax.all_to_all(
+            jnp.stack(jnp.split(gated_slots, lax.axis_size("ctx"), axis=0)), "ctx", 0, 0
+        ),
+        axis=1,
+    )
     partial_value = jnp.dot(gated_local, out_weight, preferred_element_type=jnp.float32)
     return lax.psum_scatter(partial_value, "tp", scatter_dimension=1, tiled=True).astype(
         jnp.bfloat16

time: 433 us -> 433 us (level)
  no operation moved by 1% of the time
where the time goes in v1:
time: 433 us; the launch traced here: 430 us
  local copies, waits for them, and re-layouts  305 us (70%)
  waiting for transfers between devices  39.9 us (9%)
  matrix products  23.5 us (5%)
  starting transfers between devices  20.5 us (5%)
  blocking collectives  15.1 us (3%)
  between operations  13.6 us (3%)
  other arithmetic  12.4 us (3%)
    reshape x8, local copies, waits for them, and re-layouts, skew_blocks(): return tiled.reshape(chans, blocks, 2 * blocks - 1, span)[:, :, :blocks]  103 us
    while x16, local copies, waits for them, and re-layouts  37.2 us
    reduce_scatter x1, waiting for transfers between devices, body(): lax.psum_scatter(partial_value, 'tp', scatter_dimension=1, tiled=True)  33 us
    reshape x4, local copies, waits for them, and re-layouts, skew_blocks(): tiled.reshape(chans, blocks * 2 * blocks, span)  29.3 us
    reshape x4, local copies, waits for them, and re-layouts, block_conv(): tt = tt.reshape(chans, span, blocks, span)  27.5 us
    broadcast_in_dim x20, local copies, waits for them, and re-layouts, skew_blocks(): tiled = jnp.broadcast_to(a_ext[:, None], (chans, blocks, 2 * blocks, span))  27.4 us
    reshape x4, local copies, waits for them, and re-layouts, block_conv(): tt = tt[:, :span * (width - 1)].reshape(chans, span, width - 1)[:, :, :seq]  25.7 us
    all_to_all x3, starting transfers between devices, to_channel_major(): return lax.all_to_all(a, 'ctx', 1, 0, tiled=True).T  20.5 us
  transfers between devices with their start and end apart: 4, of which 3 were waited for; matrix products, arithmetic and copies ran while one was open for 77% of the time, Pallas kernels for 0%

profile of v1, /device:TPU:1, one launch (start us, length us, event | category | flops | bytes accessed | tf_op | source)
XLA Modules:
  0.0 430.1 jit_solution(5212129369680612735)
XLA Ops:
  8.3 9.7 %all-to-all-start.1 = ((bf16[128,32,16]{0,2,1:T(8,128)(2,1)}), bf16[128,32,16]{0,2,1:T(8,128)(2,1)S(1)}, u32[]{:S(2)}, u32[]{:S(2)}) async-start(bf16[128,32,16]{0,2,1:T(8,128)(2,1)} %bitcast.15), calls=%async_computation.1 | async-start | bytes 262144 | tf_op jit(solution)/shard_map/all_to_all | solution.py:63
  25.7 6.9 %all-to-all-start.2 = ((bf16[128,32,16]{0,2,1:T(8,128)(2,1)}), bf16[128,32,16]{0,2,1:T(8,128)(2,1)S(1)}, u32[]{:S(2)}, u32[]{:S(2)}) async-start(bf16[128,32,16]{0,2,1:T(8,128)(2,1)} %bitcast.19), calls=%async_computation.2 | async-start | bytes 262144 | tf_op jit(solution)/shard_map/all_to_all | solution.py:63
  34.1 6.1 %all-to-all-done.2 = bf16[128,32,16]{0,2,1:T(8,128)(2,1)S(1)} async-done(((bf16[128,32,16]{0,2,1:T(8,128)(2,1)}), bf16[128,32,16]{0,2,1:T(8,128)(2,1)S(1)}, u32[]{:S(2)}, u32[]{:S(2)}) %all-to-all-start.2) | async-done | bytes 131104 | tf_op jit(solution)/shard_map/all_to_all | solution.py:63
  40.2 3.8 all-to-all-start
  44.2 323.0 %while.12 = (s32[]{:T(128)}, f32[4,4,4096]{2,1,0:T(4,128)}, s32[4096]{0:T(1024)S(1)}, bf16[4,4,4096]{2,1,0:T(4,128)(2,1)S(1)}, bf16[4,4,4096]{2,1,0:T(4,128)(2,1)S(1)}, /*index=5*/s32[]{:T(128)}, bf16[]{:T(256)}) while((s32[]{:T(128)}, f32[4,4,4096]{2,1,0:T(4,128)}, s32[4096]{0:T(1024)S(1)}, bf16[4,4,4096]{2,1,0:T(4,128)(2,1)S(1)}, ...), condition=%wide.region_2.4_spmd, body=%wide.region_1.0_spmd.sunk | while | flops 144167168 | bytes 68822360 | solution.py:77
  46.2 4.6 %reshape.236 = bf16[1064960]{0:T(1024)(128)(2,1)} reshape(bf16[4,64,4160]{2,1,0:T(8,128)(2,1)} %broadcast_in_dim.225) | data formatting | bytes 4259840 | tf_op jit(solution)/shard_map/while
  50.9 3.7 reshape.237
  54.6 4.5 %reshape.238 = bf16[1064704]{0:T(1024)(128)(2,1)} reshape(bf16[4,266176]{1,0:T(4,128)(2,1)} %bitcast.257) | data formatting | bytes 4258816 | tf_op jit(solution)/shard_map/while
  59.1 6.4 %reshape.239 = bf16[4,64,4159]{2,1,0:T(8,128)(2,1)} reshape(bf16[1064704]{0:T(1024)(128)(2,1)} %reshape.238) | data formatting | bytes 4258816 | tf_op jit(solution)/shard_map/while/body/eval_jaxpr/reshape | solution.py:25
  65.5 3.1 slice.80
  68.7 6.9 %reshape.240 = bf16[4,64,64,64]{3,2,1,0:T(8,128)(2,1)} reshape(bf16[4,64,4096]{2,1,0:T(8,128)(2,1)} %slice.80) | data formatting | bytes 4194304 | tf_op jit(solution)/shard_map/while/body/eval_jaxpr/reshape | solution.py:26
  80.0 7.3 %reshape.243 = bf16[4,8192,64]{1,2,0:T(8,128)(2,1)} reshape(bf16[4,64,128,64]{2,1,3,0:T(8,128)(2,1)} %broadcast_in_dim.226) | data formatting | bytes 8388608 | tf_op jit(solution)/shard_map/while/body/eval_jaxpr/reshape | solution.py:14
  87.3 19.3 %reshape.244 = bf16[4,64,127,64]{2,1,3,0:T(8,128)(2,1)} reshape(bf16[4,8128,64]{1,2,0:T(8,128)(2,1)} %bitcast.256) | data formatting | bytes 8323072 | tf_op jit(solution)/shard_map/while/body/eval_jaxpr/reshape | solution.py:15
  108.2 2.8 broadcast_in_dim.228
  111.0 6.4 %reshape.246 = s32[1,64,127,64]{2,1,3,0:T(8,128)} reshape(s32[1,8128,64]{1,2,0:T(8,128)} %bitcast.258) | data formatting | bytes 4161536 | tf_op jit(solution)/shard_map/while/body/eval_jaxpr/reshape | solution.py:15
  119.2 4.9 %fusion.52 = f32[4,64,64]{2,1,0:T(8,128)S(1)} fusion(bf16[4,64,64,64]{3,2,1,0:T(8,128)(2,1)} %reshape.240, bf16[4,64,127,64]{2,1,3,0:T(8,128)(2,1)} %reshape.244, pred[64,64,64]{1,0,2:T(8,128)(4,1)S(1)} %fusion.51, pred[64,64]{1,0:T(8,128)(4,1)S(1)} %get-tuple-element.157), kind=kOutput, calls=%fused_computation.19.clone.1 | convolution fusion | flops 135282688 | bytes 6590464 | tf_op jit(solution)/shard_map/while/body/eval_jaxpr/cjdi,cdtj->cit/dot_general | solution.py:34
  126.9 4.6 %reshape.236 = bf16[1064960]{0:T(1024)(128)(2,1)} reshape(bf16[4,64,4160]{2,1,0:T(8,128)(2,1)} %broadcast_in_dim.225) | data formatting | bytes 4259840 | tf_op jit(solution)/shard_map/while
  131.6 3.7 reshape.237
  135.3 4.5 %reshape.238 = bf16[1064704]{0:T(1024)(128)(2,1)} reshape(bf16[4,266176]{1,0:T(4,128)(2,1)} %bitcast.257) | data formatting | bytes 4258816 | tf_op jit(solution)/shard_map/while
  139.8 6.4 %reshape.239 = bf16[4,64,4159]{2,1,0:T(8,128)(2,1)} reshape(bf16[1064704]{0:T(1024)(128)(2,1)} %reshape.238) | data formatting | bytes 4258816 | tf_op jit(solution)/shard_map/while/body/eval_jaxpr/reshape | solution.py:25
  146.2 3.1 slice.80
  149.4 6.9 %reshape.240 = bf16[4,64,64,64]{3,2,1,0:T(8,128)(2,1)} reshape(bf16[4,64,4096]{2,1,0:T(8,128)(2,1)} %slice.80) | data formatting | bytes 4194304 | tf_op jit(solution)/shard_map/while/body/eval_jaxpr/reshape | solution.py:26
  160.7 7.3 %reshape.243 = bf16[4,8192,64]{1,2,0:T(8,128)(2,1)} reshape(bf16[4,64,128,64]{2,1,3,0:T(8,128)(2,1)} %broadcast_in_dim.226) | data formatting | bytes 8388608 | tf_op jit(solution)/shard_map/while/body/eval_jaxpr/reshape | solution.py:14
  168.0 19.3 %reshape.244 = bf16[4,64,127,64]{2,1,3,0:T(8,128)(2,1)} reshape(bf16[4,8128,64]{1,2,0:T(8,128)(2,1)} %bitcast.256) | data formatting | bytes 8323072 | tf_op jit(solution)/shard_map/while/body/eval_jaxpr/reshape | solution.py:15
  191.7 6.4 %reshape.246 = s32[1,64,127,64]{2,1,3,0:T(8,128)} reshape(s32[1,8128,64]{1,2,0:T(8,128)} %bitcast.258) | data formatting | bytes 4161536 | tf_op jit(solution)/shard_map/while/body/eval_jaxpr/reshape | solution.py:15
  199.9 4.9 %fusion.52 = f32[4,64,64]{2,1,0:T(8,128)S(1)} fusion(bf16[4,64,64,64]{3,2,1,0:T(8,128)(2,1)} %reshape.240, bf16[4,64,127,64]{2,1,3,0:T(8,128)(2,1)} %reshape.244, pred[64,64,64]{1,0,2:T(8,128)(4,1)S(1)} %fusion.51, pred[64,64]{1,0:T(8,128)(4,1)S(1)} %get-tuple-element.157), kind=kOutput, calls=%fused_computation.19.clone.1 | convolution fusion | flops 135282688 | bytes 6590464 | tf_op jit(solution)/shard_map/while/body/eval_jaxpr/cjdi,cdtj->cit/dot_general | solution.py:34
  207.6 4.6 %reshape.236 = bf16[1064960]{0:T(1024)(128)(2,1)} reshape(bf16[4,64,4160]{2,1,0:T(8,128)(2,1)} %broadcast_in_dim.225) | data formatting | bytes 4259840 | tf_op jit(solution)/shard_map/while
  212.2 3.7 reshape.237
  216.0 4.5 %reshape.238 = bf16[1064704]{0:T(1024)(128)(2,1)} reshape(bf16[4,266176]{1,0:T(4,128)(2,1)} %bitcast.257) | data formatting | bytes 4258816 | tf_op jit(solution)/shard_map/while
  220.5 6.4 %reshape.239 = bf16[4,64,4159]{2,1,0:T(8,128)(2,1)} reshape(bf16[1064704]{0:T(1024)(128)(2,1)} %reshape.238) | data formatting | bytes 4258816 | tf_op jit(solution)/shard_map/while/body/eval_jaxpr/reshape | solution.py:25
  226.9 3.1 slice.80
  230.1 6.9 %reshape.240 = bf16[4,64,64,64]{3,2,1,0:T(8,128)(2,1)} reshape(bf16[4,64,4096]{2,1,0:T(8,128)(2,1)} %slice.80) | data formatting | bytes 4194304 | tf_op jit(solution)/shard_map/while/body/eval_jaxpr/reshape | solution.py:26
  241.3 7.3 %reshape.243 = bf16[4,8192,64]{1,2,0:T(8,128)(2,1)} reshape(bf16[4,64,128,64]{2,1,3,0:T(8,128)(2,1)} %broadcast_in_dim.226) | data formatting | bytes 8388608 | tf_op jit(solution)/shard_map/while/body/eval_jaxpr/reshape | solution.py:14
  248.7 19.3 %reshape.244 = bf16[4,64,127,64]{2,1,3,0:T(8,128)(2,1)} reshape(bf16[4,8128,64]{1,2,0:T(8,128)(2,1)} %bitcast.256) | data formatting | bytes 8323072 | tf_op jit(solution)/shard_map/while/body/eval_jaxpr/reshape | solution.py:15
  272.3 6.4 %reshape.246 = s32[1,64,127,64]{2,1,3,0:T(8,128)} reshape(s32[1,8128,64]{1,2,0:T(8,128)} %bitcast.258) | data formatting | bytes 4161536 | tf_op jit(solution)/shard_map/while/body/eval_jaxpr/reshape | solution.py:15
  280.6 4.9 %fusion.52 = f32[4,64,64]{2,1,0:T(8,128)S(1)} fusion(bf16[4,64,64,64]{3,2,1,0:T(8,128)(2,1)} %reshape.240, bf16[4,64,127,64]{2,1,3,0:T(8,128)(2,1)} %reshape.244, pred[64,64,64]{1,0,2:T(8,128)(4,1)S(1)} %fusion.51, pred[64,64]{1,0:T(8,128)(4,1)S(1)} %get-tuple-element.157), kind=kOutput, calls=%fused_computation.19.clone.1 | convolution fusion | flops 135282688 | bytes 6590464 | tf_op jit(solution)/shard_map/while/body/eval_jaxpr/cjdi,cdtj->cit/dot_general | solution.py:34
  288.3 4.6 %reshape.236 = bf16[1064960]{0:T(1024)(128)(2,1)} reshape(bf16[4,64,4160]{2,1,0:T(8,128)(2,1)} %broadcast_in_dim.225) | data formatting | bytes 4259840 | tf_op jit(solution)/shard_map/while
  292.9 3.7 reshape.237
  296.7 4.5 %reshape.238 = bf16[1064704]{0:T(1024)(128)(2,1)} reshape(bf16[4,266176]{1,0:T(4,128)(2,1)} %bitcast.257) | data formatting | bytes 4258816 | tf_op jit(solution)/shard_map/while
  301.2 6.4 %reshape.239 = bf16[4,64,4159]{2,1,0:T(8,128)(2,1)} reshape(bf16[1064704]{0:T(1024)(128)(2,1)} %reshape.238) | data formatting | bytes 4258816 | tf_op jit(solution)/shard_map/while/body/eval_jaxpr/reshape | solution.py:25
  307.6 3.1 slice.80
  310.7 6.9 %reshape.240 = bf16[4,64,64,64]{3,2,1,0:T(8,128)(2,1)} reshape(bf16[4,64,4096]{2,1,0:T(8,128)(2,1)} %slice.80) | data formatting | bytes 4194304 | tf_op jit(solution)/shard_map/while/body/eval_jaxpr/reshape | solution.py:26
  322.0 7.3 %reshape.243 = bf16[4,8192,64]{1,2,0:T(8,128)(2,1)} reshape(bf16[4,64,128,64]{2,1,3,0:T(8,128)(2,1)} %broadcast_in_dim.226) | data formatting | bytes 8388608 | tf_op jit(solution)/shard_map/while/body/eval_jaxpr/reshape | solution.py:14
  329.4 19.3 %reshape.244 = bf16[4,64,127,64]{2,1,3,0:T(8,128)(2,1)} reshape(bf16[4,8128,64]{1,2,0:T(8,128)(2,1)} %bitcast.256) | data formatting | bytes 8323072 | tf_op jit(solution)/shard_map/while/body/eval_jaxpr/reshape | solution.py:15
  353.0 6.4 %reshape.246 = s32[1,64,127,64]{2,1,3,0:T(8,128)} reshape(s32[1,8128,64]{1,2,0:T(8,128)} %bitcast.258) | data formatting | bytes 4161536 | tf_op jit(solution)/shard_map/while/body/eval_jaxpr/reshape | solution.py:15
  361.3 4.9 %fusion.52 = f32[4,64,64]{2,1,0:T(8,128)S(1)} fusion(bf16[4,64,64,64]{3,2,1,0:T(8,128)(2,1)} %reshape.240, bf16[4,64,127,64]{2,1,3,0:T(8,128)(2,1)} %reshape.244, pred[64,64,64]{1,0,2:T(8,128)(4,1)S(1)} %fusion.51, pred[64,64]{1,0:T(8,128)(4,1)S(1)} %get-tuple-element.157), kind=kOutput, calls=%fused_computation.19.clone.1 | convolution fusion | flops 135282688 | bytes 6590464 | tf_op jit(solution)/shard_map/while/body/eval_jaxpr/cjdi,cdtj->cit/dot_general | solution.py:34
  372.1 15.1 %all_to_all.62 = bf16[32,128,16]{1,2,0:T(8,128)(2,1)S(1)} all-to-all(bf16[32,128,16]{1,2,0:T(8,128)(2,1)S(1)} %constant_dynamic-update-slice_fusion.1), channel_id=1, replica_groups=mesh['ctx'=32,'tp'=4] {'ctx'}, dimensions={0} | all-to-all | bytes 262144 | tf_op jit(solution)/shard_map/all_to_all | solution.py:87
  388.6 33.0 %reduce-scatter.2.cloned.1.call-done = f32[128,512]{1,0:T(8,128)} async-done(((f32[128,2048]{1,0:T(8,128)}), f32[128,512]{1,0:T(8,128)}) %reduce-scatter.2.cloned.1.call-update) | async-done | bytes 262160 | tf_op jit(solution)/shard_map/reduce_scatter | solution.py:93
  (176 shorter events, 69.6 us)
Async XLA Ops:
  6.5 380.6 %copy-start = (bf16[512,2048]{1,0:T(8,128)(2,1)S(1)}, bf16[512,2048]{1,0:T(8,128)(2,1)}, u32[]{:S(2)}) copy-start(bf16[512,2048]{1,0:T(8,128)(2,1)} %param.17) | copy-start | bytes 6291460
  8.3 17.3 %all-to-all-start.1 = ((bf16[128,32,16]{0,2,1:T(8,128)(2,1)}), bf16[128,32,16]{0,2,1:T(8,128)(2,1)S(1)}, u32[]{:S(2)}, u32[]{:S(2)}) async-start(bf16[128,32,16]{0,2,1:T(8,128)(2,1)} %bitcast.15), calls=%async_computation.1 | async-start | bytes 262144 | tf_op jit(solution)/shard_map/all_to_all | solution.py:63
  23.5 20.6 %copy-start.1 = (s32[4096]{0:T(1024)S(1)}, s32[4096]{0:T(1024)}, u32[]{:S(2)}) copy-start(s32[4096]{0:T(1024)} %param.15) | copy-start | bytes 49156
  25.7 14.5 %all-to-all-start.2 = ((bf16[128,32,16]{0,2,1:T(8,128)(2,1)}), bf16[128,32,16]{0,2,1:T(8,128)(2,1)S(1)}, u32[]{:S(2)}, u32[]{:S(2)}) async-start(bf16[128,32,16]{0,2,1:T(8,128)(2,1)} %bitcast.19), calls=%async_computation.2 | async-start | bytes 262144 | tf_op jit(solution)/shard_map/all_to_all | solution.py:63
  40.2 328.2 %all-to-all-start = ((bf16[128,32,16]{0,2,1:T(8,128)(2,1)}), bf16[128,32,16]{0,2,1:T(8,128)(2,1)S(1)}, u32[]{:S(2)}, u32[]{:S(2)}) async-start(bf16[128,32,16]{0,2,1:T(8,128)(2,1)} %bitcast.11), calls=%async_computation | async-start | bytes 262144 | tf_op jit(solution)/shard_map/all_to_all | solution.py:63
  44.0 377.6 %reduce-scatter.2.cloned.1.call-start = ((), (), s32[]{:S(2)}) async-start(), calls=%async_computation.5 | async-start | bytes 1310720 | tf_op jit(solution)/shard_map/reduce_scatter | solution.py:93
Sparse Core Ops, SparseCore 0:
  388.8 32.8 reduce-scatter.1
